TPU v7x, 32 devices: a whole 2x2x4 slice. The times are simulated.
32 devices in a mesh: row: 4 (over z), col: 8 (over y, x, core).
Axes of the slice: x: 2, y: 2, z: 4, core: 2. Of those that a mesh axis runs over, the one named last changes fastest.
Arguments:
- features: bfloat16 [8192, 512], P(('row', 'col')), may hold values from -6 to 6
- tile_values: bfloat16 [32, 16, 128, 128], P(('row', 'col')), may hold values from -0.21875 to 0.21875
- tile_blocks: int32 [32, 16, 2], P(('row', 'col')), may hold values from 0 to 63, as said below
- tile_count: int32 [32], P(('row', 'col')), may hold values from 1 to 16, as said below
- needed: int32 [32, 4], P(('row', 'col')), may hold values from 0 to 1
- weight_one: bfloat16 [512, 512], replicated, may hold values from -0.25 to 0.25
- weight_two: bfloat16 [512, 512], replicated, may hold values from -0.25 to 0.25
Outputs:
- nodes_out: bfloat16 [8192, 512], P(('row', 'col'))
Inputs may be any that keep to these rules, and one draw needn't show every extreme that they name: `tile_blocks`: every row block of device d lies among the row blocks owned by the devices that share its index along row; for each device e along col in device d's row, all live or dead tiles of device d whose row block is owned by e name the same one of e's 2 blocks; the last device's first slot names the last block. `tile_count`: some device in every draw has all 16 slots live.
All inputs are finite; a program needn't handle non-finite values.
Results may differ from a plain program's by a relative error of at most 0.017.
Values may be sent and summed in bfloat16 or wider, within the bound.
No kernel may reach another device: no remote copies, remote signals or barrier semaphores. Data moves between devices by JAX's collectives and lax.ppermute only.
A program may use at most 64 MiB of HBM per device.

v0:
```python
import jax
import jax.numpy as jnp
from jax import lax
from jax.sharding import PartitionSpec as P


def body(features, tile_values, tile_blocks, tile_count, needed, weight_one, weight_two):
    col_count = lax.axis_size("col")
    adjacency = tile_values[0]
    blocks_here = tile_blocks[0]
    tile_slots = adjacency.shape[0]
    tile_size = adjacency.shape[1]
    feat_width = features.shape[1]
    per_device = features.shape[0] // tile_size
    alive_mask = jnp.arange(tile_slots) < tile_count[0]
    source_owner = blocks_here[:, 1]
    wanted = needed[0]
    target = blocks_here[:, 0] // per_device % col_count
    local_block = blocks_here[:, 0] % per_device
    dest_hit = (target[:, None] == jnp.arange(col_count)[None, :]) & alive_mask[:, None]
    dest_weights = dest_hit.astype(jnp.bfloat16)
    both_weights = jnp.concatenate([dest_weights, dest_weights], axis=0)
    send_block = jnp.max(jnp.where(dest_hit, local_block[:, None], 0), axis=0)
    hidden = features
    for layer_index, weight in enumerate((weight_one, weight_two)):
        owned = hidden.reshape(per_device, tile_size, feat_width)
        panel_rows = lax.all_gather(owned, "row", axis=0, tiled=True)
        operands = panel_rows[source_owner * per_device + wanted[source_owner]]
        products = jnp.einsum(
            "tmk,tkf->tmf", adjacency, operands, preferred_element_type=jnp.float32
        )
        upper_part = products.astype(jnp.bfloat16)
        lower_part = (products - upper_part.astype(jnp.float32)).astype(jnp.bfloat16)
        stacked = jnp.concatenate([upper_part, lower_part], axis=0)
        partial_value = jnp.einsum(
            "tc,tmf->cmf", both_weights, stacked, preferred_element_type=jnp.float32
        )
        partial_value = partial_value.astype(jnp.bfloat16)
        arrived_parts = lax.all_to_all(
            partial_value, "col", split_axis=0, concat_axis=0, tiled=True
        )
        picked = lax.all_to_all(send_block, "col", split_axis=0, concat_axis=0, tiled=True)
        chooser = (picked[:, None] == jnp.arange(per_device)[None, :]).astype(jnp.bfloat16)
        summed = jnp.einsum(
            "sb,smf->bmf", chooser, arrived_parts, preferred_element_type=jnp.float32
        )
        mixed = summed.astype(jnp.bfloat16).reshape(per_device * tile_size, feat_width)
        result = jnp.dot(mixed, weight, preferred_element_type=jnp.float32)
        if layer_index == 0:
            hidden = jnp.maximum(result, 0.0).astype(jnp.bfloat16)
        else:
            hidden = result.astype(jnp.bfloat16)
    return hidden


def solution(mesh):
    placed = (
        P(("row", "col"), None),
        P(("row", "col"), None, None, None),
        P(("row", "col"), None, None),
        P(("row", "col")),
        P(("row", "col"), None),
        P(),
        P(),
    )
    return jax.shard_map(
        body, mesh=mesh, in_specs=placed, out_specs=P(("row", "col"), None), check_vma=False
    )
```

profile of v0, /device:TPU:0, one launch (start us, length us, event | category | flops | bytes accessed | tf_op | source)
XLA Modules:
  0.0 147.8 jit_solution(7393868171918821235)
XLA Ops:
  6.5 0.7 all-gather.3.cloned.1.call-update
  8.6 0.8 fusion.12
  10.2 5.2 %all-to-all-start = ((s32[8,1,1]{2,1,0:T(1,128)}), s32[8,1,1]{2,1,0:T(1,128)S(1)}, u32[]{:S(2)}, u32[]{:S(2)}) async-start(s32[8,1,1]{2,1,0:T(1,128)} %copy.23), calls=%async_computation | async-start | bytes 8192 | tf_op jit(solution)/shard_map/all_to_all | solution.py:42
  15.4 1.3 gather_fusion
  17.4 22.2 %all-gather.3.cloned.1.call-done = bf16[8,128,512]{2,1,0:T(8,128)(2,1)} async-done(((bf16[2,128,512]{2,1,0:T(8,128)(2,1)}), bf16[8,128,512]{2,1,0:T(8,128)(2,1)}) %all-gather.3.cloned.1.call-update) | async-done | bytes 1048592 | tf_op jit(solution)/shard_map/all_gather | solution.py:27
  39.6 1.9 %gather_fusion.1 = bf16[16,128,512]{2,1,0:T(8,128)(2,1)S(1)} fusion(bf16[8,128,512]{2,1,0:T(8,128)(2,1)} %all-gather.3.cloned.1.call-done, s32[1024]{0:T(1024)S(1)} %pad_clamp_fusion), kind=kCustom, calls=%fused_computation.1 | custom fusion | bytes 4194368 | tf_op jit(solution)/shard_map/gather | solution.py:28
  41.5 1.0 fusion.1
  42.5 2.3 %pad_maximum_fusion = bf16[32,128,512]{1,2,0:T(8,128)(2,1)} fusion(bf16[16,128,512]{1,2,0:T(8,128)(2,1)S(1)} %get-tuple-element.9, bf16[16,128,512]{1,2,0:T(8,128)(2,1)S(1)} %get-tuple-element.10), kind=kLoop, calls=%fused_computation.3 | loop fusion | flops 2097152 | bytes 8388608 | tf_op jit(solution)/shard_map/concatenate | solution.py:34
  44.8 8.0 %copy.25 = bf16[32,128,512]{2,0,1:T(8,128)(2,1)} copy(bf16[32,128,512]{1,2,0:T(8,128)(2,1)} %pad_maximum_fusion) | data formatting | bytes 8388608 | tf_op jit(solution)/shard_map/concatenate | solution.py:34
  52.8 2.9 %convolution_convert_fusion.1 = bf16[8,128,512]{2,0,1:T(8,128)(2,1)S(1)} fusion(bf16[32,128,512]{2,0,1:T(8,128)(2,1)} %copy.25, pred[16,8]{0,1:T(8,128)(4,1)S(1)} %fusion.9), kind=kOutput, calls=%fused_computation.12 | convolution fusion | flops 34078976 | bytes 5243008 | tf_op jit(solution)/shard_map/tc,tmf->cmf/dot_general | solution.py:35
  55.7 1.3 copy.26
  57.0 3.8 %all-to-all-start.1 = ((bf16[8,128,512]{2,1,0:T(8,128)(2,1)}), bf16[8,128,512]{2,1,0:T(8,128)(2,1)S(1)}, u32[]{:S(2)}, u32[]{:S(2)}) async-start(bf16[8,128,512]{2,1,0:T(8,128)(2,1)} %copy.26), calls=%async_computation.1 | async-start | bytes 2097152 | tf_op jit(solution)/shard_map/all_to_all | solution.py:39
  61.0 15.1 %all-to-all-done.1 = bf16[8,128,512]{2,1,0:T(8,128)(2,1)S(1)} async-done(((bf16[8,128,512]{2,1,0:T(8,128)(2,1)}), bf16[8,128,512]{2,1,0:T(8,128)(2,1)S(1)}, u32[]{:S(2)}, u32[]{:S(2)}) %all-to-all-start.1) | async-done | bytes 1048608 | tf_op jit(solution)/shard_map/all_to_all | solution.py:39
  76.2 0.7 convolution_convert_fusion.4
  77.0 1.0 fusion.2
  78.0 25.8 %all-gather.5.cloned.1.call-done = bf16[8,128,512]{2,1,0:T(8,128)(2,1)} async-done(((bf16[2,128,512]{2,1,0:T(8,128)(2,1)}), bf16[8,128,512]{2,1,0:T(8,128)(2,1)}) %all-gather.5.cloned.1.call-update) | async-done | bytes 1048592 | tf_op jit(solution)/shard_map/all_gather | solution.py:27
  103.8 1.9 %gather_fusion.2 = bf16[16,128,512]{2,1,0:T(8,128)(2,1)S(1)} fusion(bf16[8,128,512]{2,1,0:T(8,128)(2,1)} %all-gather.5.cloned.1.call-done, s32[1024]{0:T(1024)S(1)} %pad_clamp_fusion), kind=kCustom, calls=%fused_computation.2 | custom fusion | bytes 4194368 | tf_op jit(solution)/shard_map/gather | solution.py:28
  105.7 1.0 fusion
  106.7 2.3 %pad_maximum_fusion.1 = bf16[32,128,512]{1,2,0:T(8,128)(2,1)} fusion(bf16[16,128,512]{1,2,0:T(8,128)(2,1)S(1)} %get-tuple-element.5, bf16[16,128,512]{1,2,0:T(8,128)(2,1)S(1)} %get-tuple-element.6), kind=kLoop, calls=%fused_computation.4 | loop fusion | flops 2097152 | bytes 8388608 | tf_op jit(solution)/shard_map/concatenate | solution.py:34
  109.0 8.0 %copy.30 = bf16[32,128,512]{2,0,1:T(8,128)(2,1)} copy(bf16[32,128,512]{1,2,0:T(8,128)(2,1)} %pad_maximum_fusion.1) | data formatting | bytes 8388608 | tf_op jit(solution)/shard_map/concatenate | solution.py:34
  117.0 2.9 %convolution_convert_fusion = bf16[8,128,512]{2,0,1:T(8,128)(2,1)S(1)} fusion(bf16[32,128,512]{2,0,1:T(8,128)(2,1)} %copy.30, pred[16,8]{0,1:T(8,128)(4,1)S(1)} %fusion.9), kind=kOutput, calls=%fused_computation.11 | convolution fusion | flops 34078976 | bytes 5243008 | tf_op jit(solution)/shard_map/tc,tmf->cmf/dot_general | solution.py:35
  120.2 18.9 %all_to_all.20 = bf16[8,128,512]{2,1,0:T(8,128)(2,1)S(1)} all-to-all(bf16[8,128,512]{2,1,0:T(8,128)(2,1)S(1)} %copy.31), channel_id=1, replica_groups=mesh['row'=4,'col'=8] {'col'}, dimensions={0} | all-to-all | bytes 2097152 | tf_op jit(solution)/shard_map/all_to_all | solution.py:39
  139.2 0.7 convolution_convert_fusion.3
  140.0 1.0 convolution_convert_fusion.2
  (22 shorter events, 2.9 us)
Async XLA Ops:
  6.5 35.0 %copy-start = (bf16[1,16,128,128]{3,2,1,0:T(8,128)(2,1)S(1)}, bf16[1,16,128,128]{3,2,1,0:T(8,128)(2,1)}, u32[]{:S(2)}) copy-start(bf16[1,16,128,128]{3,2,1,0:T(8,128)(2,1)} %param.8) | copy-start | bytes 1572868
  6.5 33.1 %all-gather.3.cloned.1.call-start = ((), (), s32[]{:S(2)}) async-start(), calls=%async_computation.3 | async-start | bytes 1310720 | tf_op jit(solution)/shard_map/all_gather | solution.py:27
  10.2 46.8 %all-to-all-start = ((s32[8,1,1]{2,1,0:T(1,128)}), s32[8,1,1]{2,1,0:T(1,128)S(1)}, u32[]{:S(2)}, u32[]{:S(2)}) async-start(s32[8,1,1]{2,1,0:T(1,128)} %copy.23), calls=%async_computation | async-start | bytes 8192 | tf_op jit(solution)/shard_map/all_to_all | solution.py:42
  57.0 20.0 %copy-start.1 = (bf16[512,512]{1,0:T(8,128)(2,1)S(1)}, bf16[512,512]{1,0:T(8,128)(2,1)}, u32[]{:S(2)}) copy-start(bf16[512,512]{1,0:T(8,128)(2,1)} %param.12) | copy-start | bytes 1572868
  57.0 19.2 %all-to-all-start.1 = ((bf16[8,128,512]{2,1,0:T(8,128)(2,1)}), bf16[8,128,512]{2,1,0:T(8,128)(2,1)S(1)}, u32[]{:S(2)}, u32[]{:S(2)}) async-start(bf16[8,128,512]{2,1,0:T(8,128)(2,1)} %copy.26), calls=%async_computation.1 | async-start | bytes 2097152 | tf_op jit(solution)/shard_map/all_to_all | solution.py:39
  60.8 43.0 %all-gather.5.cloned.1.call-start = ((), (), s32[]{:S(2)}) async-start(), calls=%async_computation.4 | async-start | bytes 1310720 | tf_op jit(solution)/shard_map/all_gather | solution.py:27
  120.2 19.7 %copy-start.2 = (bf16[512,512]{1,0:T(8,128)(2,1)S(1)}, bf16[512,512]{1,0:T(8,128)(2,1)}, u32[]{:S(2)}) copy-start(bf16[512,512]{1,0:T(8,128)(2,1)} %param.13) | copy-start | bytes 1572868
Sparse Core Ops, SparseCore 0:
  8.9 30.6 all-gather.2
  78.1 25.6 all-gather.4
where the time goes:
time: 149 us; the launch traced here: 148 us
  waiting for transfers between devices  63.9 us (43%)
  local copies, waits for them, and re-layouts  23.4 us (16%)
  blocking collectives  18.9 us (13%)
  between operations  14.2 us (10%)
  matrix products  11.3 us (8%)
  starting transfers between devices  9 us (6%)
  other arithmetic  7.17 us (5%)
    all_gather x2, waiting for transfers between devices, body(): panel_rows = lax.all_gather(owned, 'row', axis=0, tiled=True)  48 us
    all_to_all x1, blocking collectives, body(): lax.all_to_all(partial_value, 'col', split_axis=0, concat_axis=0, tiled=T...  18.9 us
    concatenate x2, local copies, waits for them, and re-layouts, body(): stacked = jnp.concatenate([upper_part, lower_part], axis=0)  15.9 us
    all_to_all x1, waiting for transfers between devices, body(): lax.all_to_all(partial_value, 'col', split_axis=0, concat_axis=0, tiled=T...  15.1 us
    dot_general x2, matrix products, body(): jnp.einsum('tc,tmf->cmf', both_weights, stacked, preferred_element_type=j...  5.81 us
    all_to_all x1, starting transfers between devices, body(): lax.all_to_all(send_block, 'col', split_axis=0, concat_axis=0, tiled=True)  5.17 us
    gather x3, local copies, waits for them, and re-layouts, body(): operands = panel_rows[source_owner * per_device + wanted[source_owner]]  5.12 us
    concatenate x2, other arithmetic, body(): stacked = jnp.concatenate([upper_part, lower_part], axis=0)  4.64 us
  transfers between devices with their start and end apart: 4, of which 3 were waited for; matrix products, arithmetic and copies ran while one was open for 15% of the time, Pallas kernels for 0%

commit v1 on v0

--- a/solution.py
+++ b/solution.py
@@ -24,7 +24,25 @@
     hidden = features
     for layer_index, weight in enumerate((weight_one, weight_two)):
         owned = hidden.reshape(per_device, tile_size, feat_width)
-        panel_rows = lax.all_gather(owned, "row", axis=0, tiled=True)
+        ways, here, step = (lax.axis_size("row"), lax.axis_index("row"), owned.shape[0])
+        dims = [n * ways if d == 0 else n for d, n in enumerate(owned.shape)]
+        full = lax.dynamic_update_slice_in_dim(
+            jnp.zeros(dims, owned.dtype), owned, here * step, axis=0
+        )
+        going_up = going_down = owned
+        for far in range(1, ways // 2 + 1):
+            going_up = lax.ppermute(going_up, "row", [(d, (d + 1) % ways) for d in range(ways)])
+            full = lax.dynamic_update_slice_in_dim(
+                full, going_up, (here - far) % ways * step, axis=0
+            )
+            if 2 * far < ways:
+                going_down = lax.ppermute(
+                    going_down, "row", [(d, (d - 1) % ways) for d in range(ways)]
+                )
+                full = lax.dynamic_update_slice_in_dim(
+                    full, going_down, (here + far) % ways * step, axis=0
+                )
+        panel_rows = full
         operands = panel_rows[source_owner * per_device + wanted[source_owner]]
         products = jnp.einsum(
             "tmk,tkf->tmf", adjacency, operands, preferred_element_type=jnp.float32

time: 149 us -> 124 us (0.83)
  waiting for transfers between devices: 63.9 us -> 40.9 us
  between operations: 14.2 us -> 0.94 us
  starting transfers between devices: 9 us -> 16.9 us
  matrix products: 11.3 us -> 13.7 us
  local copies, waits for them, and re-layouts: 23.4 us -> 24.9 us
    all_gather x2 -> x0, waiting for transfers between devices: 48 us -> none  [body(): panel_rows = lax.all_gather(owned, 'row', axis=0, tiled=True)]
    ppermute x0 -> x6, waiting for transfers between devices: none -> 25.7 us  [the longest x4 22.5 us: body(): lax.ppermute(going_up, 'row', [(d, (d + 1) % ways) for d in range(ways)])]
    ppermute x0 -> x6, starting transfers between devices: none -> 9.04 us  [the longest x2 5.89 us: body(): lax.ppermute(going_down, 'row', [(d, (d - 1) % ways) for d in range(ways)])]
    dot_general x2, matrix products: 1.94 us -> 5.12 us  [body(): jnp.einsum('tmk,tkf->tmf', adjacency, operands, preferred_element_type=jn...]
  transfers between devices with their start and end apart: 4 -> 8, of which waited for: 3 -> 6; matrix products, arithmetic and copies ran while one was open for 15% -> 20% of each run, Pallas kernels for 0% -> 0%
where the time goes in v1:
time: 124 us
  waiting for transfers between devices  40.9 us (33%)
  local copies, waits for them, and re-layouts  24.9 us (20%)
  blocking collectives  19.1 us (15%)
  starting transfers between devices  16.9 us (14%)
  matrix products  13.7 us (11%)
  other arithmetic  7.16 us (6%)
    ppermute x4, waiting for transfers between devices, body(): lax.ppermute(going_up, 'row', [(d, (d + 1) % ways) for d in range(ways)])  22.5 us
    all_to_all x1, blocking collectives, body(): lax.all_to_all(partial_value, 'col', split_axis=0, concat_axis=0, tiled=T...  19.1 us
    concatenate x2, local copies, waits for them, and re-layouts, body(): stacked = jnp.concatenate([upper_part, lower_part], axis=0)  15.9 us
    all_to_all x1, waiting for transfers between devices, body(): lax.all_to_all(partial_value, 'col', split_axis=0, concat_axis=0, tiled=T...  15.2 us
    ppermute x2, starting transfers between devices, body(): lax.ppermute(going_down, 'row', [(d, (d - 1) % ways) for d in range(ways)])  5.89 us
    dot_general x2, matrix products, body(): jnp.einsum('tc,tmf->cmf', both_weights, stacked, preferred_element_type=j...  5.81 us
    gather x3, local copies, waits for them, and re-layouts, body(): operands = panel_rows[source_owner * per_device + wanted[source_owner]]  5.34 us
    dot_general x2, matrix products, body(): jnp.einsum('tmk,tkf->tmf', adjacency, operands, preferred_element_type=jn...  5.12 us
  transfers between devices with their start and end apart: 8, of which 6 were waited for; matrix products, arithmetic and copies ran while one was open for 20% of the time, Pallas kernels for 0%

profile of v1, /device:TPU:0, one launch (start us, length us, event | category | flops | bytes accessed | tf_op | source)
XLA Modules:
  0.0 123.6 jit_solution(3990507002772194064)
XLA Ops:
  0.0 3.0 %collective-permute-start = (bf16[2,128,512]{2,1,0:T(8,128)(2,1)}, bf16[2,128,512]{2,1,0:T(8,128)(2,1)S(1)}, u32[]{:S(2)}, u32[]{:S(2)}) collective-permute-start(bf16[2,128,512]{2,1,0:T(8,128)(2,1)} %bitcast.65), channel_id=1, source_target_pairs={{0,8},{8,16},{16,24},{24,0},{1,9},{9,17},{17,25},{25,1},{2,10},{10... | collective-permute-start | bytes 786440 | tf_op jit(solution)/shard_map/ppermute | solution.py:34
  3.0 2.1 %collective-permute-start.1 = (bf16[2,128,512]{2,1,0:T(8,128)(2,1)}, bf16[2,128,512]{2,1,0:T(8,128)(2,1)S(1)}, u32[]{:S(2)}, u32[]{:S(2)}) collective-permute-start(bf16[2,128,512]{2,1,0:T(8,128)(2,1)} %bitcast.66), channel_id=1, source_target_pairs={{0,24},{8,0},{16,8},{24,16},{1,25},{9,1},{17,9},{25,17},{2,26},{10... | collective-permute-start | bytes 786440 | tf_op jit(solution)/shard_map/ppermute | solution.py:39
  8.0 3.9 %all-to-all-start = ((s32[8,1,1]{2,1,0:T(1,128)}), s32[8,1,1]{2,1,0:T(1,128)S(1)}, u32[]{:S(2)}, u32[]{:S(2)}) async-start(s32[8,1,1]{2,1,0:T(1,128)} %copy.23), calls=%async_computation | async-start | bytes 8192 | tf_op jit(solution)/shard_map/all_to_all | solution.py:60
  11.9 1.3 %gather_fusion = s32[16]{0:T(128)S(1)} fusion(s32[4]{0:T(128)} %bitcast.59, s32[1024]{0:T(1024)S(1)} %pad_clamp_fusion.1), kind=kCustom, calls=%fused_computation | custom fusion | bytes 192 | tf_op jit(solution)/shard_map/gather | solution.py:46
  15.2 1.4 %collective-permute-done.1 = bf16[2,128,512]{2,1,0:T(8,128)(2,1)S(1)} collective-permute-done((bf16[2,128,512]{2,1,0:T(8,128)(2,1)}, bf16[2,128,512]{2,1,0:T(8,128)(2,1)S(1)}, u32[]{:S(2)}, u32[]{:S(2)}) %collective-permute-start.1) | collective-permute-done | bytes 262176 | tf_op jit(solution)/shard_map/ppermute | solution.py:39
  16.6 9.0 %collective-permute-done.2 = bf16[2,128,512]{2,1,0:T(8,128)(2,1)S(1)} collective-permute-done((bf16[2,128,512]{2,1,0:T(8,128)(2,1)S(1)}, bf16[2,128,512]{2,1,0:T(8,128)(2,1)S(1)}, u32[]{:S(2)}, u32[]{:S(2)}) %collective-permute-start.2) | collective-permute-done | bytes 262176 | tf_op jit(solution)/shard_map/ppermute | solution.py:34
  25.6 2.0 %gather_fusion.1 = bf16[16,128,512]{2,1,0:T(8,128)(2,1)} fusion(bf16[8,128,512]{2,1,0:T(8,128)(2,1)S(1)} %constant_dynamic-update-slice_fusion.4, s32[1024]{0:T(1024)S(1)} %pad_clamp_fusion), kind=kCustom, calls=%fused_computation.1 | custom fusion | bytes 4194368 | tf_op jit(solution)/shard_map/gather | solution.py:46
  27.6 2.6 %fusion.1 = (bf16[16,128,512]{1,2,0:T(8,128)(2,1)S(1)}, bf16[16,128,512]{1,2,0:T(8,128)(2,1)S(1)}) fusion(bf16[16,128,512]{2,1,0:T(8,128)(2,1)} %gather_fusion.1, bf16[1,16,128,128]{3,2,1,0:T(8,128)(2,1)S(1)} %copy-done), kind=kOutput, calls=%fused_computation.10 | convolution fusion | flops 272629760 | bytes 6815744 | tf_op jit(solution)/shard_map/tmk,tkf->tmf/dot_general | solution.py:47
  30.2 2.3 %pad_maximum_fusion = bf16[32,128,512]{1,2,0:T(8,128)(2,1)} fusion(bf16[16,128,512]{1,2,0:T(8,128)(2,1)S(1)} %get-tuple-element.9, bf16[16,128,512]{1,2,0:T(8,128)(2,1)S(1)} %get-tuple-element.10), kind=kLoop, calls=%fused_computation.3 | loop fusion | flops 2097152 | bytes 8388608 | tf_op jit(solution)/shard_map/concatenate | solution.py:52
  32.5 8.0 %copy.25 = bf16[32,128,512]{2,0,1:T(8,128)(2,1)} copy(bf16[32,128,512]{1,2,0:T(8,128)(2,1)} %pad_maximum_fusion) | data formatting | bytes 8388608 | tf_op jit(solution)/shard_map/concatenate | solution.py:52
  40.5 2.9 %convolution_convert_fusion.1 = bf16[8,128,512]{2,0,1:T(8,128)(2,1)S(1)} fusion(bf16[32,128,512]{2,0,1:T(8,128)(2,1)} %copy.25, pred[16,8]{0,1:T(8,128)(4,1)S(1)} %fusion.9), kind=kOutput, calls=%fused_computation.12 | convolution fusion | flops 34078976 | bytes 5243008 | tf_op jit(solution)/shard_map/tc,tmf->cmf/dot_general | solution.py:53
  43.4 1.3 %copy.26 = bf16[8,128,512]{2,1,0:T(8,128)(2,1)} copy(bf16[8,128,512]{2,0,1:T(8,128)(2,1)S(1)} %convolution_convert_fusion.1) | data formatting | bytes 2097152 | tf_op jit(solution)/shard_map/convert_element_type | solution.py:56
  44.7 4.0 %all-to-all-start.1 = ((bf16[8,128,512]{2,1,0:T(8,128)(2,1)}), bf16[8,128,512]{2,1,0:T(8,128)(2,1)S(1)}, u32[]{:S(2)}, u32[]{:S(2)}) async-start(bf16[8,128,512]{2,1,0:T(8,128)(2,1)} %copy.26), calls=%async_computation.1 | async-start | bytes 2097152 | tf_op jit(solution)/shard_map/all_to_all | solution.py:57
  48.9 15.2 %all-to-all-done.1 = bf16[8,128,512]{2,1,0:T(8,128)(2,1)S(1)} async-done(((bf16[8,128,512]{2,1,0:T(8,128)(2,1)}), bf16[8,128,512]{2,1,0:T(8,128)(2,1)S(1)}, u32[]{:S(2)}, u32[]{:S(2)}) %all-to-all-start.1) | async-done | bytes 1048608 | tf_op jit(solution)/shard_map/all_to_all | solution.py:57
  65.2 3.8 %collective-permute-start.4 = (bf16[2,128,512]{2,1,0:T(8,128)(2,1)S(1)}, bf16[2,128,512]{2,1,0:T(8,128)(2,1)S(1)}, u32[]{:S(2)}, u32[]{:S(2)}) collective-permute-start(bf16[2,128,512]{2,1,0:T(8,128)(2,1)S(1)} %bitcast.61), channel_id=1, source_target_pairs={{0,24},{8,0},{16,8},{24,16},{1,25},{9,1},{17,9},{25,17},{2,26},{10... | collective-permute-start | bytes 786440 | tf_op jit(solution)/shard_map/ppermute | solution.py:39
  69.1 7.3 %collective-permute-done.3 = bf16[2,128,512]{2,1,0:T(8,128)(2,1)S(1)} collective-permute-done((bf16[2,128,512]{2,1,0:T(8,128)(2,1)S(1)}, bf16[2,128,512]{2,1,0:T(8,128)(2,1)S(1)}, u32[]{:S(2)}, u32[]{:S(2)}) %collective-permute-start.3) | collective-permute-done | bytes 262176 | tf_op jit(solution)/shard_map/ppermute | solution.py:34
  76.5 1.7 %collective-permute-done.4 = bf16[2,128,512]{2,1,0:T(8,128)(2,1)S(1)} collective-permute-done((bf16[2,128,512]{2,1,0:T(8,128)(2,1)S(1)}, bf16[2,128,512]{2,1,0:T(8,128)(2,1)S(1)}, u32[]{:S(2)}, u32[]{:S(2)}) %collective-permute-start.4) | collective-permute-done | bytes 262176 | tf_op jit(solution)/shard_map/ppermute | solution.py:39
  78.3 6.2 %collective-permute-done.5 = bf16[2,128,512]{2,1,0:T(8,128)(2,1)S(1)} collective-permute-done((bf16[2,128,512]{2,1,0:T(8,128)(2,1)S(1)}, bf16[2,128,512]{2,1,0:T(8,128)(2,1)S(1)}, u32[]{:S(2)}, u32[]{:S(2)}) %collective-permute-start.5) | collective-permute-done | bytes 262176 | tf_op jit(solution)/shard_map/ppermute | solution.py:34
  84.6 2.0 %gather_fusion.2 = bf16[16,128,512]{2,1,0:T(8,128)(2,1)} fusion(bf16[8,128,512]{2,1,0:T(8,128)(2,1)S(1)} %constant_dynamic-update-slice_fusion, s32[1024]{0:T(1024)S(1)} %pad_clamp_fusion), kind=kCustom, calls=%fused_computation.2 | custom fusion | bytes 4194368 | tf_op jit(solution)/shard_map/gather | solution.py:46
  86.6 2.6 %fusion = (bf16[16,128,512]{1,2,0:T(8,128)(2,1)S(1)}, bf16[16,128,512]{1,2,0:T(8,128)(2,1)S(1)}) fusion(bf16[16,128,512]{2,1,0:T(8,128)(2,1)} %gather_fusion.2, bf16[1,16,128,128]{3,2,1,0:T(8,128)(2,1)S(1)} %copy-done), kind=kOutput, calls=%fused_computation.7 | convolution fusion | flops 272629760 | bytes 6815744 | tf_op jit(solution)/shard_map/tmk,tkf->tmf/dot_general | solution.py:47
  89.2 2.3 %pad_maximum_fusion.1 = bf16[32,128,512]{1,2,0:T(8,128)(2,1)} fusion(bf16[16,128,512]{1,2,0:T(8,128)(2,1)S(1)} %get-tuple-element.5, bf16[16,128,512]{1,2,0:T(8,128)(2,1)S(1)} %get-tuple-element.6), kind=kLoop, calls=%fused_computation.4 | loop fusion | flops 2097152 | bytes 8388608 | tf_op jit(solution)/shard_map/concatenate | solution.py:52
  91.5 8.0 %copy.30 = bf16[32,128,512]{2,0,1:T(8,128)(2,1)} copy(bf16[32,128,512]{1,2,0:T(8,128)(2,1)} %pad_maximum_fusion.1) | data formatting | bytes 8388608 | tf_op jit(solution)/shard_map/concatenate | solution.py:52
  99.4 2.9 %convolution_convert_fusion = bf16[8,128,512]{2,0,1:T(8,128)(2,1)S(1)} fusion(bf16[32,128,512]{2,0,1:T(8,128)(2,1)} %copy.30, pred[16,8]{0,1:T(8,128)(4,1)S(1)} %fusion.9), kind=kOutput, calls=%fused_computation.11 | convolution fusion | flops 34078976 | bytes 5243008 | tf_op jit(solution)/shard_map/tc,tmf->cmf/dot_general | solution.py:53
  102.7 19.1 %all_to_all.20 = bf16[8,128,512]{2,1,0:T(8,128)(2,1)S(1)} all-to-all(bf16[8,128,512]{2,1,0:T(8,128)(2,1)S(1)} %copy.31), channel_id=1, replica_groups=mesh['row'=4,'col'=8] {'col'}, dimensions={0} | all-to-all | bytes 2097152 | tf_op jit(solution)/shard_map/all_to_all | solution.py:57
  (38 shorter events, 7.8 us)
Async XLA Ops:
  0.0 27.6 %copy-start = (bf16[1,16,128,128]{3,2,1,0:T(8,128)(2,1)S(1)}, bf16[1,16,128,128]{3,2,1,0:T(8,128)(2,1)}, u32[]{:S(2)}) copy-start(bf16[1,16,128,128]{3,2,1,0:T(8,128)(2,1)} %param.8) | copy-start | bytes 1572868
  0.0 15.0 %collective-permute-start = (bf16[2,128,512]{2,1,0:T(8,128)(2,1)}, bf16[2,128,512]{2,1,0:T(8,128)(2,1)S(1)}, u32[]{:S(2)}, u32[]{:S(2)}) collective-permute-start(bf16[2,128,512]{2,1,0:T(8,128)(2,1)} %bitcast.65), channel_id=1, source_target_pairs={{0,8},{8,16},{16,24},{24,0},{1,9},{9,17},{17,25},{25,1},{2,10},{10... | collective-permute-start | bytes 786440 | tf_op jit(solution)/shard_map/ppermute | solution.py:34
  3.0 13.6 %collective-permute-start.1 = (bf16[2,128,512]{2,1,0:T(8,128)(2,1)}, bf16[2,128,512]{2,1,0:T(8,128)(2,1)S(1)}, u32[]{:S(2)}, u32[]{:S(2)}) collective-permute-start(bf16[2,128,512]{2,1,0:T(8,128)(2,1)} %bitcast.66), channel_id=1, source_target_pairs={{0,24},{8,0},{16,8},{24,16},{1,25},{9,1},{17,9},{25,17},{2,26},{10... | collective-permute-start | bytes 786440 | tf_op jit(solution)/shard_map/ppermute | solution.py:39
  8.0 36.7 %all-to-all-start = ((s32[8,1,1]{2,1,0:T(1,128)}), s32[8,1,1]{2,1,0:T(1,128)S(1)}, u32[]{:S(2)}, u32[]{:S(2)}) async-start(s32[8,1,1]{2,1,0:T(1,128)} %copy.23), calls=%async_computation | async-start | bytes 8192 | tf_op jit(solution)/shard_map/all_to_all | solution.py:60
  15.0 10.6 %collective-permute-start.2 = (bf16[2,128,512]{2,1,0:T(8,128)(2,1)S(1)}, bf16[2,128,512]{2,1,0:T(8,128)(2,1)S(1)}, u32[]{:S(2)}, u32[]{:S(2)}) collective-permute-start(bf16[2,128,512]{2,1,0:T(8,128)(2,1)S(1)} %collective-permute-done), channel_id=1, source_target_pairs={{0,8},{8,16},{16,24},{24,0},{1,9},{9,17},{17,25},{25,1},{2,10},{10... | collective-permute-start | bytes 786440 | tf_op jit(solution)/shard_map/ppermute | solution.py:34
  44.7 20.2 %copy-start.1 = (bf16[512,512]{1,0:T(8,128)(2,1)S(1)}, bf16[512,512]{1,0:T(8,128)(2,1)}, u32[]{:S(2)}) copy-start(bf16[512,512]{1,0:T(8,128)(2,1)} %param.12) | copy-start | bytes 1572868
  44.7 19.4 %all-to-all-start.1 = ((bf16[8,128,512]{2,1,0:T(8,128)(2,1)}), bf16[8,128,512]{2,1,0:T(8,128)(2,1)S(1)}, u32[]{:S(2)}, u32[]{:S(2)}) async-start(bf16[8,128,512]{2,1,0:T(8,128)(2,1)} %copy.26), calls=%async_computation.1 | async-start | bytes 2097152 | tf_op jit(solution)/shard_map/all_to_all | solution.py:57
  65.2 11.2 %collective-permute-start.3 = (bf16[2,128,512]{2,1,0:T(8,128)(2,1)S(1)}, bf16[2,128,512]{2,1,0:T(8,128)(2,1)S(1)}, u32[]{:S(2)}, u32[]{:S(2)}) collective-permute-start(bf16[2,128,512]{2,1,0:T(8,128)(2,1)S(1)} %bitcast.60), channel_id=1, source_target_pairs={{0,8},{8,16},{16,24},{24,0},{1,9},{9,17},{17,25},{25,1},{2,10},{10... | collective-permute-start | bytes 786440 | tf_op jit(solution)/shard_map/ppermute | solution.py:34
  65.2 13.0 %collective-permute-start.4 = (bf16[2,128,512]{2,1,0:T(8,128)(2,1)S(1)}, bf16[2,128,512]{2,1,0:T(8,128)(2,1)S(1)}, u32[]{:S(2)}, u32[]{:S(2)}) collective-permute-start(bf16[2,128,512]{2,1,0:T(8,128)(2,1)S(1)} %bitcast.61), channel_id=1, source_target_pairs={{0,24},{8,0},{16,8},{24,16},{1,25},{9,1},{17,9},{25,17},{2,26},{10... | collective-permute-start | bytes 786440 | tf_op jit(solution)/shard_map/ppermute | solution.py:39
  76.4 8.2 %collective-permute-start.5 = (bf16[2,128,512]{2,1,0:T(8,128)(2,1)S(1)}, bf16[2,128,512]{2,1,0:T(8,128)(2,1)S(1)}, u32[]{:S(2)}, u32[]{:S(2)}) collective-permute-start(bf16[2,128,512]{2,1,0:T(8,128)(2,1)S(1)} %collective-permute-done.3), channel_id=1, source_target_pairs={{0,8},{8,16},{16,24},{24,0},{1,9},{9,17},{17,25},{25,1},{2,10},{10... | collective-permute-start | bytes 786440 | tf_op jit(solution)/shard_map/ppermute | solution.py:34
  102.7 19.9 %copy-start.2 = (bf16[512,512]{1,0:T(8,128)(2,1)S(1)}, bf16[512,512]{1,0:T(8,128)(2,1)}, u32[]{:S(2)}) copy-start(bf16[512,512]{1,0:T(8,128)(2,1)} %param.13) | copy-start | bytes 1572868
